TPU v7x, 512 devices: a whole 4x4x16 slice. The times are simulated.
512 devices in a mesh: sector: 16 (over y, x_lo, core), dom: 32 (over z, x_hi).
Axes of the slice: x: 4 (x_hi: 2, x_lo: 2; x = x_hi * 2 + x_lo), y: 4, z: 16, core: 2. Of those that a mesh axis runs over, the one named last changes fastest.
Arguments:
- amplitudes: float32 [64, 48], replicated, may hold values from -0.3 to 0.3
- mode_shapes: float32 [48, 3, 524288], P(None, None, ('sector', 'dom')), may hold values from -6 to 6
- shape_grads: float32 [8, 3, 524288], P(None, None, ('sector', 'dom')), may hold values from -2.4 to 2.4
- lame_params: float32 [2, 524288], P(None, ('sector', 'dom')), may hold values from 0.5 to 2
- connectivity: int32 [8, 524288], P(None, ('sector', 'dom')), may hold values from -1 to 1791, as said below
- dom_sends: int32 [2, 131072], P(None, ('sector', 'dom')), may hold values from -1 to 1023, as said below
- sector_sends: int32 [2, 65536], P(None, ('sector', 'dom')), may hold values from -1 to 1023, as said below
Outputs:
- nodal_force: float32 [64, 3, 524288], P(None, None, ('sector', 'dom'))
- modal_force: float32 [64, 48], replicated
Inputs may be any that keep to these rules, and one draw needn't show every extreme that they name: `connectivity`: in each device's block, the live elements come first and the padding element slots after them hold -1 in all 8 rows; a live slot names a slot of the device's extended table. Some device has all 1024 slots live. `dom_sends`: each device's row lists its own node numbers first, then -1; a row holds 128 to 256 live entries, and some row is full. `sector_sends`: each device's row lists its own node numbers first, then -1; a row holds 64 to 128 live entries, and some row is full.
All inputs are finite; a program needn't handle non-finite values.
Results may differ from a plain program's by a relative error of at most 0.0003.
Values sent between devices are 32-bit elements; how exact they have to be, the bound alone decides.
A program may use at most 64 MiB of HBM per device.

v0:
```python
import math
import jax
import jax.numpy as jnp
from jax import lax
from jax.sharding import PartitionSpec as P


def padded(cells, sides, width, closed):
    for axis, dim in sides:
        count = lax.axis_size(axis)
        ends = count if closed else count - 1
        head = lax.slice_in_dim(cells, 0, width, axis=dim)
        tail = lax.slice_in_dim(cells, cells.shape[dim] - width, cells.shape[dim], axis=dim)
        cells = jnp.concatenate(
            [
                lax.ppermute(tail, axis, [(i, (i + 1) % count) for i in range(ends)]),
                cells,
                lax.ppermute(head, axis, [((i + 1) % count, i) for i in range(ends)]),
            ],
            axis=dim,
        )
    return cells


def take_slots(node_table, send_lists):
    slot_width = node_table.shape[1]
    slot_index = jnp.where(send_lists < 0, slot_width, send_lists).reshape(-1)
    return jnp.take(node_table, slot_index, axis=1, mode="fill", fill_value=0.0)


def add_slots(node_table, send_lists, add_values):
    slot_width = node_table.shape[1]
    slot_index = jnp.where(send_lists < 0, slot_width, send_lists).reshape(-1)
    return node_table.at[:, slot_index].add(add_values, mode="drop")


def element_forces(accum, extended, connect, gradients, lame):
    ext_width = extended.shape[1]
    combo_total = extended.shape[0] // 3
    elem_total = connect.shape[1]
    slot_index = jnp.where(connect < 0, ext_width, connect).reshape(-1)
    corners = jnp.take(extended, slot_index, axis=1, mode="fill", fill_value=0.0).reshape(
        combo_total, 3, 8, elem_total
    )
    gradient = jnp.zeros((combo_total, 3, 3, elem_total), extended.dtype)
    for corner in range(8):
        gradient = gradient + corners[:, :, None, corner, :] * gradients[corner][None, None, :, :]
    quadratic = jnp.sum(gradient[:, :, :, None, :] * gradient[:, :, None, :, :], axis=1)
    green_strain = 0.5 * (gradient + jnp.swapaxes(gradient, 1, 2) + quadratic)
    strain_trace = green_strain[:, 0, 0] + green_strain[:, 1, 1] + green_strain[:, 2, 2]
    identity = jnp.eye(3, dtype=extended.dtype)[None, :, :, None]
    stress = lame[0] * strain_trace[:, None, None, :] * identity + 2.0 * lame[1] * green_strain
    piola = stress + jnp.sum(gradient[:, :, :, None, :] * stress[:, None, :, :, :], axis=2)
    corner_forces = jnp.stack(
        [jnp.sum(piola * gradients[corner][None, None, :, :], axis=2) for corner in range(8)],
        axis=2,
    )
    return accum.at[:, slot_index].add(
        corner_forces.reshape(3 * combo_total, 8 * elem_total), mode="drop"
    )


def outer_ends(ext_rows, slot_width):
    return jnp.concatenate([ext_rows[:, :slot_width], ext_rows[:, 3 * slot_width :]], axis=1)


def local(amplitudes, mode_shapes, shape_grads, lame_params, connectivity, dom_sends, sector_sends):
    modes_total, _, node_total = mode_shapes.shape
    combo_total = amplitudes.shape[0]
    table_rows = 3 * combo_total
    dom_width = dom_sends.shape[1]
    sec_width = sector_sends.shape[1]
    flat_shapes = mode_shapes.reshape(modes_total, 3 * node_total)
    displaced = jnp.dot(
        amplitudes, flat_shapes, precision=lax.Precision.HIGHEST, preferred_element_type=jnp.float32
    ).reshape(table_rows, node_total)
    dom_ext = padded(take_slots(displaced, dom_sends), (("dom", 1),), dom_width, False)
    sec_ext = padded(take_slots(displaced, sector_sends), (("sector", 1),), sec_width, True)
    halo_moved = jnp.concatenate(
        [outer_ends(dom_ext, dom_width), outer_ends(sec_ext, sec_width)], axis=1
    )
    extended = jnp.concatenate([displaced, halo_moved], axis=1)
    ext_width = extended.shape[1]
    elem_total = connectivity.shape[1]
    block_size = math.gcd(elem_total, 256)
    turn_total = elem_total // block_size

    def one_block(turn_index, forces):
        first_col = turn_index * block_size
        connect_block = lax.dynamic_slice_in_dim(connectivity, first_col, block_size, 1)
        grads_block = lax.dynamic_slice_in_dim(shape_grads, first_col, block_size, 2)
        lame_block = lax.dynamic_slice_in_dim(lame_params, first_col, block_size, 1)
        return element_forces(forces, extended, connect_block, grads_block, lame_block)

    slot_forces = lax.fori_loop(
        0, turn_total, one_block, jnp.zeros((table_rows, ext_width), jnp.float32)
    )
    own_forces = slot_forces[:, :node_total]
    dom_back = slot_forces[:, node_total : node_total + 2 * dom_width]
    sec_back = slot_forces[:, node_total + 2 * dom_width :]
    dom_return = padded(dom_back, (("dom", 1),), dom_width, False)
    own_forces = add_slots(own_forces, dom_sends, outer_ends(dom_return, dom_width))
    sec_return = padded(sec_back, (("sector", 1),), sec_width, True)
    own_forces = add_slots(own_forces, sector_sends, outer_ends(sec_return, sec_width))
    partial_modal = lax.dot_general(
        own_forces.reshape(combo_total, 3 * node_total),
        flat_shapes,
        (((1,), (1,)), ((), ())),
        precision=lax.Precision.HIGHEST,
        preferred_element_type=jnp.float32,
    )
    modal_total = lax.psum(partial_modal, ("sector", "dom"))
    all_nodes = node_total * lax.axis_size("sector") * lax.axis_size("dom")
    return (
        own_forces.reshape(combo_total, 3, node_total),
        modal_total / math.sqrt(3.0 * all_nodes),
    )


def solution(mesh):
    placed = (
        P(),
        P(None, None, ("sector", "dom")),
        P(None, None, ("sector", "dom")),
        P(None, ("sector", "dom")),
        P(None, ("sector", "dom")),
        P(None, ("sector", "dom")),
        P(None, ("sector", "dom")),
    )
    return jax.shard_map(
        local,
        mesh=mesh,
        in_specs=placed,
        out_specs=(P(None, None, ("sector", "dom")), P()),
        check_vma=False,
    )
```

profile of v0, /device:TPU:1, one launch (start us, length us, event | category | flops | bytes accessed | tf_op | source)
XLA Modules:
  0.0 308.0 jit_solution(2652404135059010113)
XLA Ops:
  2.1 1.1 copy.105
  5.3 1.6 gather_fusion.1
  7.1 5.5 %collective-permute-start = (f32[192,256]{0,1:T(8,128)S(1)}, f32[192,256]{0,1:T(8,128)S(1)}, u32[]{:S(2)}, u32[]{:S(2)}) collective-permute-start(f32[192,256]{0,1:T(8,128)S(1)} %get-tuple-element.244), channel_id=1, source_target_pairs={{0,1},{1,2},{2,3},{3,4},{4,5},{5,6},{6,7},{7,8},{8,9},{9,10},{10,1... | collective-permute-start | bytes 589832 | tf_op jit(solution)/shard_map/ppermute | solution.py:16
  12.6 1.0 gather_fusion.2
  13.7 4.6 %collective-permute-start.3 = (f32[192,128]{0,1:T(8,128)S(1)}, f32[192,128]{0,1:T(8,128)S(1)}, u32[]{:S(2)}, u32[]{:S(2)}) collective-permute-start(f32[192,128]{0,1:T(8,128)S(1)} %get-tuple-element.245), channel_id=1, source_target_pairs={{32,0},{64,32},{96,64},{128,96},{160,128},{192,160},{224,192},{256... | collective-permute-start | bytes 294920 | tf_op jit(solution)/shard_map/ppermute | solution.py:18
  18.4 1.9 collective-permute-start.2
  20.3 1.5 collective-permute-start.1
  21.9 9.2 %collective-permute-done.1 = f32[192,256]{0,1:T(8,128)S(1)} collective-permute-done((f32[192,256]{0,1:T(8,128)S(1)}, f32[192,256]{0,1:T(8,128)S(1)}, u32[]{:S(2)}, u32[]{:S(2)}) %collective-permute-start.1) | collective-permute-done | bytes 196640 | tf_op jit(solution)/shard_map/ppermute | solution.py:18
  31.3 1.1 copy-done.1
  32.4 136.4 %while.15 = (s32[]{:T(128)}, f32[192,1792]{0,1:T(8,128)S(1)}, s32[8,1024]{1,0:T(8,128)S(1)}, f32[2,1024]{1,0:T(2,128)}, f32[192,1792]{0,1:T(8,128)}, /*index=5*/...) while((s32[]{:T(128)}, f32[192,1792]{0,1:T(8,128)S(1)}, ...), condition=%wide.region_12.13_spmd, body=%wide.region_0.12_spmd.sunk | while | flops 12415007 | bytes 49229240 | solution.py:95
  33.3 1.3 constant_dynamic-slice_fusion.11
  34.6 10.1 %gather_fusion = f32[2048,192]{1,0:T(8,128)} fusion(f32[192,1792]{0,1:T(8,128)} %get-tuple-element.414, s32[2048]{0:T(1024)S(1)} %broadcast_clamp_fusion.2), kind=kCustom, calls=%fused_computation.clone.1 | custom fusion | bytes 3153920 | tf_op jit(solution)/shard_map/while/body/eval_jaxpr/jit(_take)/gather | solution.py:42
  44.7 1.9 copy.147
  47.3 1.1 fusion.28
  50.4 0.9 copy.149
  51.9 1.8 copy.151
  53.8 12.6 %scatter_fusion = f32[192,1792]{0,1:T(8,128)S(1)} fusion(f32[192,1792]{0,1:T(8,128)S(1)} %get-tuple-element.394, s32[2048]{0:T(1024)S(1)} %bitcast.158, f32[2048,192]{1,0:T(8,128)} %copy.151), kind=kCustom, calls=%fused_computation.3.clone.1 | custom fusion | flops 393216 | bytes 4726784 | tf_op jit(solution)/shard_map/while/body/eval_jaxpr/scatter-add | solution.py:58
  67.4 1.4 constant_dynamic-slice_fusion.11
  68.8 10.1 %gather_fusion = f32[2048,192]{1,0:T(8,128)} fusion(f32[192,1792]{0,1:T(8,128)} %get-tuple-element.414, s32[2048]{0:T(1024)S(1)} %broadcast_clamp_fusion.2), kind=kCustom, calls=%fused_computation.clone.1 | custom fusion | bytes 3153920 | tf_op jit(solution)/shard_map/while/body/eval_jaxpr/jit(_take)/gather | solution.py:42
  78.8 1.9 copy.147
  81.4 1.1 fusion.28
  84.5 0.9 copy.149
  86.0 1.8 copy.151
  87.9 12.6 %scatter_fusion = f32[192,1792]{0,1:T(8,128)S(1)} fusion(f32[192,1792]{0,1:T(8,128)S(1)} %get-tuple-element.394, s32[2048]{0:T(1024)S(1)} %bitcast.158, f32[2048,192]{1,0:T(8,128)} %copy.151), kind=kCustom, calls=%fused_computation.3.clone.1 | custom fusion | flops 393216 | bytes 4726784 | tf_op jit(solution)/shard_map/while/body/eval_jaxpr/scatter-add | solution.py:58
  101.5 1.3 constant_dynamic-slice_fusion.11
  102.8 10.1 %gather_fusion = f32[2048,192]{1,0:T(8,128)} fusion(f32[192,1792]{0,1:T(8,128)} %get-tuple-element.414, s32[2048]{0:T(1024)S(1)} %broadcast_clamp_fusion.2), kind=kCustom, calls=%fused_computation.clone.1 | custom fusion | bytes 3153920 | tf_op jit(solution)/shard_map/while/body/eval_jaxpr/jit(_take)/gather | solution.py:42
  112.9 1.9 copy.147
  115.5 1.1 fusion.28
  118.6 0.9 copy.149
  120.1 1.8 copy.151
  122.0 12.6 %scatter_fusion = f32[192,1792]{0,1:T(8,128)S(1)} fusion(f32[192,1792]{0,1:T(8,128)S(1)} %get-tuple-element.394, s32[2048]{0:T(1024)S(1)} %bitcast.158, f32[2048,192]{1,0:T(8,128)} %copy.151), kind=kCustom, calls=%fused_computation.3.clone.1 | custom fusion | flops 393216 | bytes 4726784 | tf_op jit(solution)/shard_map/while/body/eval_jaxpr/scatter-add | solution.py:58
  135.6 1.4 constant_dynamic-slice_fusion.11
  137.0 10.1 %gather_fusion = f32[2048,192]{1,0:T(8,128)} fusion(f32[192,1792]{0,1:T(8,128)} %get-tuple-element.414, s32[2048]{0:T(1024)S(1)} %broadcast_clamp_fusion.2), kind=kCustom, calls=%fused_computation.clone.1 | custom fusion | bytes 3153920 | tf_op jit(solution)/shard_map/while/body/eval_jaxpr/jit(_take)/gather | solution.py:42
  147.0 1.9 copy.147
  149.6 1.1 fusion.28
  152.7 0.9 copy.149
  154.2 1.8 copy.151
  156.1 12.6 %scatter_fusion = f32[192,1792]{0,1:T(8,128)S(1)} fusion(f32[192,1792]{0,1:T(8,128)S(1)} %get-tuple-element.394, s32[2048]{0:T(1024)S(1)} %bitcast.158, f32[2048,192]{1,0:T(8,128)} %copy.151), kind=kCustom, calls=%fused_computation.3.clone.1 | custom fusion | flops 393216 | bytes 4726784 | tf_op jit(solution)/shard_map/while/body/eval_jaxpr/scatter-add | solution.py:58
  168.8 2.8 collective-permute-start.4
  171.6 1.3 collective-permute-start.5
  173.6 4.8 %collective-permute-start.6 = (f32[192,128]{0,1:T(8,128)}, f32[192,128]{0,1:T(8,128)}, u32[]{:S(2)}, u32[]{:S(2)}) collective-permute-start(f32[192,128]{0,1:T(8,128)} %get-tuple-element.239), channel_id=1, source_target_pairs={{0,32},{32,64},{64,96},{96,128},{128,160},{160,192},{192,224},{224... | collective-permute-start | bytes 294920 | tf_op jit(solution)/shard_map/ppermute | solution.py:16
  178.4 2.2 collective-permute-start.7
  180.7 3.8 %scatter_custom_fusion.1 = f32[192,1024]{0,1:T(8,128)S(1)} fusion(f32[192,1024]{0,1:T(8,128)S(1)} %slice.257, s32[512]{0:T(512)S(1)} %bitcast.167, f32[192,256]{0,1:T(8,128)S(1)} %collective-permute-done.5, f32[]{:T(128)} %constant.154, f32[192,256]{0,1:T(8,128)S(1)} %collective-permute-done.4), kind=kCustom, calls=%fused_computation.67 | custom fusion | flops 196608 | bytes 1310724 | tf_op jit(solution)/shard_map/scatter-add | solution.py:34
  184.5 0.9 collective-permute-done.6
  185.4 4.3 %collective-permute-done.7 = f32[192,128]{0,1:T(8,128)} collective-permute-done((f32[192,128]{0,1:T(8,128)}, f32[192,128]{0,1:T(8,128)}, u32[]{:S(2)}, u32[]{:S(2)}) %collective-permute-start.7) | collective-permute-done | bytes 98336 | tf_op jit(solution)/shard_map/ppermute | solution.py:18
  189.6 3.0 scatter_custom_fusion.2
  194.8 111.2 %psum.7 = f32[64,48]{0,1:T(8,128)S(1)} all-reduce(f32[64,48]{0,1:T(8,128)S(1)} %fusion.18), channel_id=1, replica_groups=mesh['sector'=16,'dom'=32] {'sector','dom'}, use_global_device_ids=true, to_apply=%region_15.16 | all-reduce | flops 3072 | bytes 24576 | tf_op jit(solution)/shard_map/psum | solution.py:112
  306.6 1.3 copy.92
  (178 shorter events, 24.1 us)
Async XLA Ops:
  0.6 3.4 %copy-start = (f32[64,48]{0,1:T(8,128)S(1)}, f32[64,48]{0,1:T(8,128)}, u32[]{:S(2)}) copy-start(f32[64,48]{0,1:T(8,128)} %param.9) | copy-start | bytes 36868
  3.2 0.8 copy-start.2
  6.9 5.7 %copy-start.5 = (s32[2,128]{1,0:T(2,128)S(1)}, s32[2,128]{1,0:T(2,128)}, u32[]{:S(2)}) copy-start(s32[2,128]{1,0:T(2,128)} %param.15) | copy-start | bytes 3076
  7.1 14.8 %collective-permute-start = (f32[192,256]{0,1:T(8,128)S(1)}, f32[192,256]{0,1:T(8,128)S(1)}, u32[]{:S(2)}, u32[]{:S(2)}) collective-permute-start(f32[192,256]{0,1:T(8,128)S(1)} %get-tuple-element.244), channel_id=1, source_target_pairs={{0,1},{1,2},{2,3},{3,4},{4,5},{5,6},{6,7},{7,8},{8,9},{9,10},{10,1... | collective-permute-start | bytes 589832 | tf_op jit(solution)/shard_map/ppermute | solution.py:16
  13.7 17.4 %collective-permute-start.3 = (f32[192,128]{0,1:T(8,128)S(1)}, f32[192,128]{0,1:T(8,128)S(1)}, u32[]{:S(2)}, u32[]{:S(2)}) collective-permute-start(f32[192,128]{0,1:T(8,128)S(1)} %get-tuple-element.245), channel_id=1, source_target_pairs={{32,0},{64,32},{96,64},{128,96},{160,128},{192,160},{224,192},{256... | collective-permute-start | bytes 294920 | tf_op jit(solution)/shard_map/ppermute | solution.py:18
  18.4 12.7 %collective-permute-start.2 = (f32[192,128]{0,1:T(8,128)S(1)}, f32[192,128]{0,1:T(8,128)S(1)}, u32[]{:S(2)}, u32[]{:S(2)}) collective-permute-start(f32[192,128]{0,1:T(8,128)S(1)} %get-tuple-element.246), channel_id=1, source_target_pairs={{0,32},{32,64},{64,96},{96,128},{128,160},{160,192},{192,224},{224... | collective-permute-start | bytes 294920 | tf_op jit(solution)/shard_map/ppermute | solution.py:16
  20.3 10.8 %collective-permute-start.1 = (f32[192,256]{0,1:T(8,128)S(1)}, f32[192,256]{0,1:T(8,128)S(1)}, u32[]{:S(2)}, u32[]{:S(2)}) collective-permute-start(f32[192,256]{0,1:T(8,128)S(1)} %get-tuple-element.243), channel_id=1, source_target_pairs={{1,0},{2,1},{3,2},{4,3},{5,4},{6,5},{7,6},{8,7},{9,8},{10,9},{11,1... | collective-permute-start | bytes 589832 | tf_op jit(solution)/shard_map/ppermute | solution.py:18
  21.9 10.5 %copy-start.4 = (s32[8,1024]{1,0:T(8,128)S(1)}, s32[8,1024]{1,0:T(8,128)}, u32[]{:S(2)}) copy-start(s32[8,1024]{1,0:T(8,128)} %param.13) | copy-start | bytes 98308
  31.1 1.2 copy-start.1
  168.8 11.9 %collective-permute-start.4 = (f32[192,256]{0,1:T(8,128)S(1)}, f32[192,256]{0,1:T(8,128)S(1)}, u32[]{:S(2)}, u32[]{:S(2)}) collective-permute-start(f32[192,256]{0,1:T(8,128)S(1)} %get-tuple-element.241), channel_id=1, source_target_pairs={{0,1},{1,2},{2,3},{3,4},{4,5},{5,6},{6,7},{7,8},{8,9},{9,10},{10,1... | collective-permute-start | bytes 589832 | tf_op jit(solution)/shard_map/ppermute | solution.py:16
  171.6 9.1 %collective-permute-start.5 = (f32[192,256]{0,1:T(8,128)S(1)}, f32[192,256]{0,1:T(8,128)S(1)}, u32[]{:S(2)}, u32[]{:S(2)}) collective-permute-start(f32[192,256]{0,1:T(8,128)S(1)} %get-tuple-element.242), channel_id=1, source_target_pairs={{1,0},{2,1},{3,2},{4,3},{5,4},{6,5},{7,6},{8,7},{9,8},{10,9},{11,1... | collective-permute-start | bytes 589832 | tf_op jit(solution)/shard_map/ppermute | solution.py:18
  173.6 11.8 %collective-permute-start.6 = (f32[192,128]{0,1:T(8,128)}, f32[192,128]{0,1:T(8,128)}, u32[]{:S(2)}, u32[]{:S(2)}) collective-permute-start(f32[192,128]{0,1:T(8,128)} %get-tuple-element.239), channel_id=1, source_target_pairs={{0,32},{32,64},{64,96},{96,128},{128,160},{160,192},{192,224},{224... | collective-permute-start | bytes 294920 | tf_op jit(solution)/shard_map/ppermute | solution.py:16
  178.4 11.3 %collective-permute-start.7 = (f32[192,128]{0,1:T(8,128)}, f32[192,128]{0,1:T(8,128)}, u32[]{:S(2)}, u32[]{:S(2)}) collective-permute-start(f32[192,128]{0,1:T(8,128)} %get-tuple-element.240), channel_id=1, source_target_pairs={{32,0},{64,32},{96,64},{128,96},{160,128},{192,160},{224,192},{256... | collective-permute-start | bytes 294920 | tf_op jit(solution)/shard_map/ppermute | solution.py:18
  193.0 1.1 copy-start.3
where the time goes:
time: 309 us; the launch traced here: 308 us
  blocking collectives  111 us (36%)
  local copies, waits for them, and re-layouts  87.5 us (28%)
  other arithmetic  66.7 us (22%)
  starting transfers between devices  24.6 us (8%)
  waiting for transfers between devices  14.3 us (5%)
    psum x1, blocking collectives, local(): modal_total = lax.psum(partial_modal, ('sector', 'dom'))  111 us
    scatter-add x4, other arithmetic, element_forces(): accum.at[:, slot_index]  50.6 us
    gather x8, local copies, waits for them, and re-layouts, element_forces(): jnp.take(extended, slot_index, axis=1, mode='fill', fill_value=0.0)  47.8 us
    ppermute x4, starting transfers between devices, padded(): lax.ppermute(tail, axis, [(i, (i + 1) % count) for i in range(ends)])  15 us
    ppermute x4, waiting for transfers between devices, padded(): lax.ppermute(head, axis, [((i + 1) % count, i) for i in range(ends)])  13.4 us
    ppermute x4, starting transfers between devices, padded(): lax.ppermute(head, axis, [((i + 1) % count, i) for i in range(ends)])  9.62 us
    reshape x4, local copies, waits for them, and re-layouts, element_forces(): corner_forces.reshape(3 * combo_total, 8 * elem_total)  7.39 us
    scatter-add x2, other arithmetic, add_slots(): return node_table.at[:, slot_index].add(add_values, mode='drop')  6.78 us
  transfers between devices with their start and end apart: 8, of which 3 were waited for; matrix products, arithmetic and copies ran while one was open for 2% of the time, Pallas kernels for 0%

commit v1 on v0

--- a/solution.py
+++ b/solution.py
@@ -109,7 +109,8 @@
         precision=lax.Precision.HIGHEST,
         preferred_element_type=jnp.float32,
     )
-    modal_total = lax.psum(partial_modal, ("sector", "dom"))
+    pieces = lax.all_gather(partial_modal, ("sector", "dom"), axis=0, tiled=False)
+    modal_total = pieces.sum(axis=0)
     all_nodes = node_total * lax.axis_size("sector") * lax.axis_size("dom")
     return (
         own_forces.reshape(combo_total, 3, node_total),

time: 309 us -> 1650 us (5.34)
  waiting for transfers between devices: 14.3 us -> 1450 us
  blocking collectives: 111 us -> 0 us
    all_gather x0 -> x1, waiting for transfers between devices: none -> 1430 us  [local(): lax.all_gather(partial_modal, ('sector', 'dom'), axis=0, tiled=False)]
    psum x1 -> x0, blocking collectives: 111 us -> none  [local(): modal_total = lax.psum(partial_modal, ('sector', 'dom'))]
  transfers between devices with their start and end apart: 8 -> 9, of which waited for: 3 -> 4; matrix products, arithmetic and copies ran while one was open for 2% -> 1% of each run, Pallas kernels for 0% -> 0%
where the time goes in v1:
time: 1650 us
  waiting for transfers between devices  1450 us (88%)
  local copies, waits for them, and re-layouts  89.2 us (5%)
  other arithmetic  72.2 us (4%)
  starting transfers between devices  24.6 us (1%)
    all_gather x1, waiting for transfers between devices, local(): lax.all_gather(partial_modal, ('sector', 'dom'), axis=0, tiled=False)  1430 us
    scatter-add x4, other arithmetic, element_forces(): accum.at[:, slot_index]  50.6 us
    gather x8, local copies, waits for them, and re-layouts, element_forces(): jnp.take(extended, slot_index, axis=1, mode='fill', fill_value=0.0)  47.8 us
  transfers between devices with their start and end apart: 9, of which 4 were waited for; matrix products, arithmetic and copies ran while one was open for 1% of the time, Pallas kernels for 0%

profile of v1, /device:TPU:1, one launch (start us, length us, event | category | flops | bytes accessed | tf_op | source)
XLA Modules:
  0.0 1649.3 jit_solution(5571730572772006597)
XLA Ops:
  8.6 1.1 copy.140
  11.1 1.6 gather_fusion.1
  12.9 5.5 collective-permute-start
  18.4 1.0 gather_fusion.2
  19.5 4.6 collective-permute-start.3
  24.2 1.9 collective-permute-start.2
  26.1 1.5 collective-permute-start.1
  27.6 1.1 constant_dynamic-update-slice_fusion.4
  29.4 7.5 collective-permute-done.1
  39.0 136.3 %while.15 = (s32[]{:T(128)}, f32[192,1792]{0,1:T(8,128)S(1)}, s32[8,1024]{1,0:T(8,128)S(1)}, f32[2,1024]{1,0:T(2,128)}, f32[192,1792]{0,1:T(8,128)}, /*index=5*/...) while((s32[]{:T(128)}, f32[192,1792]{0,1:T(8,128)S(1)}, ...), condition=%wide.region_12.13_spmd, body=%wide.region_0.12_spmd.sunk | while | flops 12415007 | bytes 49229240 | solution.py:95
  40.0 1.3 constant_dynamic-slice_fusion.11
  41.4 10.1 gather_fusion
  51.4 1.9 copy.182
  54.0 1.1 fusion.27
  57.1 0.9 copy.184
  58.6 1.8 copy.186
  60.5 12.6 scatter_fusion
  74.1 1.4 constant_dynamic-slice_fusion.11
  75.5 10.1 gather_fusion
  85.5 1.9 copy.182
  88.2 1.1 fusion.27
  91.2 0.9 copy.184
  92.8 1.8 copy.186
  94.6 12.6 scatter_fusion
  108.2 1.4 constant_dynamic-slice_fusion.11
  109.6 10.1 gather_fusion
  119.7 1.9 copy.182
  122.3 1.1 fusion.27
  126.9 1.8 copy.186
  128.7 12.6 scatter_fusion
  142.3 1.2 constant_dynamic-slice_fusion.11
  143.5 10.1 gather_fusion
  153.6 1.9 copy.182
  156.2 1.1 fusion.27
  159.3 0.9 copy.184
  160.8 1.8 copy.186
  162.7 12.6 scatter_fusion
  175.4 2.8 collective-permute-start.4
  178.2 1.3 collective-permute-start.5
  180.2 4.8 collective-permute-start.6
  185.0 2.2 collective-permute-start.7
  187.3 3.8 scatter_custom_fusion.1
  192.0 4.3 collective-permute-done.7
  196.2 3.0 scatter_custom_fusion.2
  200.3 1.4 convolution_bitcast_fusion
  202.0 1.3 copy.127
  203.4 1433.0 %all-gather.4.cloned.1.call-done = f32[512,64,48]{1,2,0:T(8,128)} async-done(((f32[1,64,48]{1,2,0:T(8,128)}), f32[512,64,48]{1,2,0:T(8,128)}) %all-gather.4.cloned.1.call-update) | async-done | bytes 6291472 | tf_op jit(solution)/shard_map/all_gather | solution.py:112
  1636.4 5.5 reduce_sum.169
  (179 shorter events, 27.0 us)
Async XLA Ops:
  7.2 2.6 copy-start
  7.2 1629.2 %all-gather.4.cloned.1.call-start = ((), (), s32[]{:S(2)}) async-start(), calls=%async_computation | async-start | bytes 12607488 | tf_op jit(solution)/shard_map/all_gather | solution.py:112
  9.8 0.8 copy-start.1
  12.7 5.7 copy-start.4
  12.9 15.7 collective-permute-start
  19.5 18.7 %collective-permute-start.3 = (f32[192,128]{0,1:T(8,128)S(1)}, f32[192,128]{0,1:T(8,128)S(1)}, u32[]{:S(2)}, u32[]{:S(2)}) collective-permute-start(f32[192,128]{0,1:T(8,128)S(1)} %get-tuple-element.253), channel_id=1, source_target_pairs={{32,0},{64,32},{96,64},{128,96},{160,128},{192,160},{224,192},{256... | collective-permute-start | bytes 294920 | tf_op jit(solution)/shard_map/ppermute | solution.py:18
  24.2 13.4 collective-permute-start.2
  26.1 10.8 collective-permute-start.1
  28.6 10.4 copy-start.3
  175.4 11.9 collective-permute-start.4
  178.2 9.1 collective-permute-start.5
  180.2 11.8 collective-permute-start.6
  185.0 11.3 collective-permute-start.7
  199.2 1.1 copy-start.2
Sparse Core Ops, SparseCore 0:
  201.8 1434.4 all-gather.3
